TPU v7x, 256 devices: a whole 4x4x8 slice. The times are simulated.
256 devices in a mesh: gy: 64 (over x, y, z_hi, core), gz: 4 (over z_lo).
Axes of the slice: x: 4, y: 4, z: 8 (z_hi: 2, z_lo: 4; z = z_hi * 4 + z_lo), core: 2. Of those that a mesh axis runs over, the one named last changes fastest.
Arguments:
- efield_check: bfloat16 [3, 2048, 8, 1024], P(None, 'gy', None, 'gz'), may hold values from -6 to 6
- hfield_check: bfloat16 [3, 2048, 8, 1024], P(None, 'gy', None, 'gz'), may hold values from -6 to 6
- polar_check: bfloat16 [3, 2048, 8, 1024], P(None, 'gy', None, 'gz'), may hold values from -4 to 4
- rate_check: bfloat16 [3, 2048, 8, 1024], P(None, 'gy', None, 'gz'), may hold values from -4 to 4
- levels_check: bfloat16 [2, 2048, 8, 1024], P(None, 'gy', None, 'gz'), may hold values from 0.049804688 to 0.5
- efield_seed: float32 [3, 2048, 8, 1024], P(None, 'gy', None, 'gz'), may hold values from -6 to 6
- hfield_seed: float32 [3, 2048, 8, 1024], P(None, 'gy', None, 'gz'), may hold values from -6 to 6
- polar_seed: float32 [3, 2048, 8, 1024], P(None, 'gy', None, 'gz'), may hold values from -6 to 6
- rate_seed: float32 [3, 2048, 8, 1024], P(None, 'gy', None, 'gz'), may hold values from -6 to 6
- levels_seed: float32 [2, 2048, 8, 1024], P(None, 'gy', None, 'gz'), may hold values from -6 to 6
- material_labels: int32 [2048, 8, 1024], P('gy', None, 'gz'), may hold values from 0 to 3
- gain_labels: int32 [2048, 8, 1024], P('gy', None, 'gz'), may hold values 0 or 1
- inverse_table: float32 [4], replicated, may hold values from 0.08 to 1
- source_field: float32 [2048, 8, 1024], P('gy', None, 'gz'), may hold values from -6 to 6
- start_step: int32 [1], replicated, may hold values from 0 to 255
Outputs:
- efield_grad: float32 [3, 2048, 8, 1024], P(None, 'gy', None, 'gz')
- hfield_grad: float32 [3, 2048, 8, 1024], P(None, 'gy', None, 'gz')
- polar_grad: float32 [3, 2048, 8, 1024], P(None, 'gy', None, 'gz')
- rate_grad: float32 [3, 2048, 8, 1024], P(None, 'gy', None, 'gz')
- levels_grad: float32 [2, 2048, 8, 1024], P(None, 'gy', None, 'gz')
- cell_grad: float32 [2048, 8, 1024], P('gy', None, 'gz')
- table_grad: float32 [4], replicated
All inputs are finite; a program needn't handle non-finite values. No bound on the sum of `gain_labels` on one device may be relied on, other than what follows from the above.
Results may differ from a plain program's by a relative error of at most 0.0003.
Values may be sent and summed in bfloat16 or wider, within the bound.
No kernel may reach another device: no remote copies, remote signals or barrier semaphores. Data moves between devices by JAX's collectives and lax.ppermute only.
A program may use at most 64 MiB of HBM per device.

v0:
```python
import math
import jax
import jax.numpy as jnp
from jax import lax
from jax.sharding import PartitionSpec as P

MAGNETIC_STEP = 0.5
ELECTRIC_STEP = 0.5
TIME_STEP = 0.5
DAMPING = 0.9
STIFFNESS = 0.3
COUPLING = 0.4
PUMPING = 0.05
UPPER_DECAY = 0.02
LOWER_DECAY = 0.3
STIMULATED = 0.2
SOURCE_OMEGA = 0.35


def shifted(block, axis, distance):
    devices = range(lax.axis_size(axis))
    route = [(i - distance, i) for i in devices if i - distance in devices]
    return lax.ppermute(block, axis, route)


def front(values, axis):
    rest = lax.slice_in_dim(values, 1, values.shape[axis], axis=axis)
    border = jnp.zeros_like(lax.slice_in_dim(values, 0, 1, axis=axis))
    return jnp.concatenate([rest, border], axis)


def behind(values, axis):
    rest = lax.slice_in_dim(values, 0, values.shape[axis] - 1, axis=axis)
    border = jnp.zeros_like(lax.slice_in_dim(values, 0, 1, axis=axis))
    return jnp.concatenate([border, rest], axis)


def curl_from(along_x, along_y, along_z):
    return jnp.stack([along_y[2] - along_z[1], along_z[0] - along_x[2], along_x[1] - along_y[0]])


def curl_forward(field):
    front_row = shifted(field[:, :1], "gy", -1)
    front_column = shifted(field[:, :, :, :1], "gz", -1)
    along_y = jnp.concatenate([field[:, 1:], front_row], 1) - field
    along_z = jnp.concatenate([field[:, :, :, 1:], front_column], 3) - field
    along_x = front(field, 2) - field
    return curl_from(along_x, along_y, along_z)


def curl_backward(field):
    back_row = shifted(field[:, -1:], "gy", 1)
    back_column = shifted(field[:, :, :, -1:], "gz", 1)
    along_y = field - jnp.concatenate([back_row, field[:, :-1]], 1)
    along_z = field - jnp.concatenate([back_column, field[:, :, :, :-1]], 3)
    along_x = field - behind(field, 2)
    return curl_from(along_x, along_y, along_z)


def local_update(
    efield, polar_field, polar_rate, levels, curl_field, inverse, gain_region, source_push
):
    rate_next = (
        DAMPING * polar_rate
        - STIFFNESS * polar_field
        + COUPLING * gain_region * (levels[0] - levels[1]) * efield
    )
    polar_next = polar_field + TIME_STEP * rate_next
    forcing = ELECTRIC_STEP * curl_field - (polar_next - polar_field)
    forcing = jnp.concatenate([forcing[:2], forcing[2:] - source_push[None]], 0)
    efield_next = efield + inverse * forcing
    stimulated = STIMULATED * gain_region * jnp.sum(efield_next * rate_next, axis=0)
    upper = (
        levels[0]
        + TIME_STEP * (PUMPING * (1.0 - levels[0] - levels[1]) - UPPER_DECAY * levels[0])
        - stimulated
    )
    lower = levels[1] + TIME_STEP * (UPPER_DECAY * levels[0] - LOWER_DECAY * levels[1]) + stimulated
    return (efield_next, polar_next, rate_next, jnp.stack([upper, lower]))


def reverse_local(
    efield, polar_field, polar_rate, levels, curl_field, inverse, gain_region, source_push, seeds
):

    def update(first, second, third, fourth, fifth, sixth):
        return local_update(first, second, third, fourth, fifth, sixth, gain_region, source_push)

    unused, pullback = jax.vjp(update, efield, polar_field, polar_rate, levels, curl_field, inverse)
    return pullback(seeds)


def material_map(material_labels, inverse_table):
    inverse = jnp.zeros(material_labels.shape, jnp.float32)
    for label in range(inverse_table.shape[0]):
        inverse = inverse + jnp.where(
            material_labels == label, inverse_table[label], jnp.float32(0.0)
        )
    return inverse


def label_sums(material_labels, values, count):
    return jnp.stack(
        [
            jnp.sum(jnp.where(material_labels == label, values, jnp.float32(0.0)))
            for label in range(count)
        ]
    )


def step_total(material_labels, values, count):
    return lax.psum(label_sums(material_labels, values, count), ("gy", "gz"))


def on_device(
    efield_check,
    hfield_check,
    polar_check,
    rate_check,
    levels_check,
    efield_seed,
    hfield_seed,
    polar_seed,
    rate_seed,
    levels_seed,
    material_labels,
    gain_labels,
    inverse_table,
    source_field,
    start_step,
):
    count = inverse_table.shape[0]
    inverse = material_map(material_labels, inverse_table)
    gain_region = gain_labels.astype(jnp.float32)
    start = start_step[0].astype(jnp.float32)
    first_sine = jnp.sin(SOURCE_OMEGA * start)
    push_first = first_sine * source_field
    push_second = jnp.sin(SOURCE_OMEGA * (start + 1.0)) * source_field
    efield = efield_check.astype(jnp.float32)
    polar_field = polar_check.astype(jnp.float32)
    polar_rate = rate_check.astype(jnp.float32)
    levels = levels_check.astype(jnp.float32)
    hfield = hfield_check.astype(jnp.float32)
    hfield_mid = hfield - MAGNETIC_STEP * curl_forward(efield)
    curl_first = curl_backward(hfield_mid)
    state_one = local_update(
        efield, polar_field, polar_rate, levels, curl_first, inverse, gain_region, push_first
    )
    hfield_next = hfield_mid - MAGNETIC_STEP * curl_forward(state_one[0])
    curl_second = curl_backward(hfield_next)
    back_e, back_p, back_q, back_n, back_c, grad_second = reverse_local(
        state_one[0],
        state_one[1],
        state_one[2],
        state_one[3],
        curl_second,
        inverse,
        gain_region,
        push_second,
        (efield_seed, polar_seed, rate_seed, levels_seed),
    )
    h_back = hfield_seed + curl_forward(back_c)
    e_back = back_e - MAGNETIC_STEP * curl_backward(h_back)
    last_e, polar_grad, rate_grad, levels_grad, last_c, grad_first = reverse_local(
        efield,
        polar_field,
        polar_rate,
        levels,
        curl_first,
        inverse,
        gain_region,
        push_first,
        (e_back, back_p, back_q, back_n),
    )
    hfield_grad = h_back + curl_forward(last_c)
    efield_grad = last_e - MAGNETIC_STEP * curl_backward(hfield_grad)
    cell_grad = grad_second + grad_first
    cells = (
        material_labels.shape[0]
        * material_labels.shape[1]
        * material_labels.shape[2]
        * lax.axis_size("gy")
        * lax.axis_size("gz")
    )
    totals = step_total(material_labels, grad_second, count) + step_total(
        material_labels, grad_first, count
    )
    table_grad = totals * (1.0 / math.sqrt(cells))
    return (efield_grad, hfield_grad, polar_grad, rate_grad, levels_grad, cell_grad, table_grad)


def solution(mesh):
    placed = (
        P(None, "gy", None, "gz"),
        P(None, "gy", None, "gz"),
        P(None, "gy", None, "gz"),
        P(None, "gy", None, "gz"),
        P(None, "gy", None, "gz"),
        P(None, "gy", None, "gz"),
        P(None, "gy", None, "gz"),
        P(None, "gy", None, "gz"),
        P(None, "gy", None, "gz"),
        P(None, "gy", None, "gz"),
        P("gy", None, "gz"),
        P("gy", None, "gz"),
        P(),
        P("gy", None, "gz"),
        P(),
    )
    return jax.shard_map(
        on_device,
        mesh=mesh,
        in_specs=placed,
        out_specs=(
            P(None, "gy", None, "gz"),
            P(None, "gy", None, "gz"),
            P(None, "gy", None, "gz"),
            P(None, "gy", None, "gz"),
            P(None, "gy", None, "gz"),
            P("gy", None, "gz"),
            P(),
        ),
        check_vma=False,
    )
```

profile of v0, /device:TPU:2, one launch (start us, length us, event | category | flops | bytes accessed | tf_op | source)
XLA Modules:
  0.0 215.5 jit_solution(16821565105719444470)
XLA Ops:
  1.7 1.3 collective-permute-start.1
  3.0 11.0 %collective-permute-start = (f32[3,1,8,256]{3,2,1,0:T(8,128)S(1)}, f32[3,1,8,256]{3,2,1,0:T(8,128)S(1)}, u32[]{:S(2)}, u32[]{:S(2)}) collective-permute-start(f32[3,1,8,256]{3,2,1,0:T(8,128)S(1)} %slice.410), channel_id=1, source_target_pairs={{4,0},{8,4},{12,8},{16,12},{20,16},{24,20},{28,24},{32,28},{36,32}... | collective-permute-start | bytes 73736 | tf_op jit(solution)/shard_map/ppermute | solution.py:23
  17.4 4.3 %collective-permute-start.3 = (f32[3,32,8,1]{3,2,1,0:T(8,128)S(1)}, f32[3,32,8,1]{3,2,1,0:T(8,128)S(1)}, u32[]{:S(2)}, u32[]{:S(2)}) collective-permute-start(f32[3,32,8,1]{3,2,1,0:T(8,128)S(1)} %slice.423), channel_id=1, source_target_pairs={{0,1},{1,2},{2,3},{4,5},{5,6},{6,7},{8,9},{9,10},{10,11},{12,13},{... | collective-permute-start | bytes 9224 | tf_op jit(solution)/shard_map/ppermute | solution.py:23
  21.7 5.1 %collective-permute-start.2 = (f32[3,1,8,256]{3,2,1,0:T(8,128)S(1)}, f32[3,1,8,256]{3,2,1,0:T(8,128)S(1)}, u32[]{:S(2)}, u32[]{:S(2)}) collective-permute-start(f32[3,1,8,256]{3,2,1,0:T(8,128)S(1)} %slice.420), channel_id=1, source_target_pairs={{0,4},{4,8},{8,12},{12,16},{16,20},{20,24},{24,28},{28,32},{32,36}... | collective-permute-start | bytes 73736 | tf_op jit(solution)/shard_map/ppermute | solution.py:23
  26.8 2.8 %select_add_fusion.2 = (f32[32,8,256]{2,1,0:T(8,128)S(1)}, pred[32,8,256]{2,1,0:T(8,128)(4,1)S(1)}, pred[32,8,256]{2,1,0:T(8,128)(4,1)S(1)}, pred[32,8,256]{2,1,...) fusion(f32[]{:T(128)} %bitcast.6, f32[]{:T(128)} %bitcast.5, f32[]{:T(128)} %bitcast.4, ...), kind=kLoop, calls=%fused_computation.118 | loop fusion | flops 983040 | bytes 1835024 | tf_op jit(solution)/shard_map/add | solution.py:96
  30.5 8.8 %collective-permute-done.2 = f32[3,1,8,256]{3,2,1,0:T(8,128)S(1)} collective-permute-done((f32[3,1,8,256]{3,2,1,0:T(8,128)S(1)}, f32[3,1,8,256]{3,2,1,0:T(8,128)S(1)}, u32[]{:S(2)}, u32[]{:S(2)}) %collective-permute-start.2) | collective-permute-done | bytes 24608 | tf_op jit(solution)/shard_map/ppermute | solution.py:23
  42.5 1.4 collective-permute-start.5
  43.9 1.9 collective-permute-start.4
  46.5 5.8 %collective-permute-done.5 = f32[3,32,8,1]{3,2,1,0:T(8,128)S(1)} collective-permute-done((f32[3,32,8,1]{3,2,1,0:T(8,128)S(1)}, f32[3,32,8,1]{3,2,1,0:T(8,128)S(1)}, u32[]{:S(2)}, u32[]{:S(2)}) %collective-permute-start.5) | collective-permute-done | bytes 3104 | tf_op jit(solution)/shard_map/ppermute | solution.py:23
  53.0 2.0 collective-permute-start.7
  55.0 1.9 collective-permute-start.6
  57.2 5.5 %collective-permute-done.7 = f32[3,32,8,1]{3,2,1,0:T(8,128)S(1)} collective-permute-done((f32[3,32,8,1]{3,2,1,0:T(8,128)S(1)}, f32[3,32,8,1]{3,2,1,0:T(8,128)S(1)}, u32[]{:S(2)}, u32[]{:S(2)}) %collective-permute-start.7) | collective-permute-done | bytes 3104 | tf_op jit(solution)/shard_map/ppermute | solution.py:23
  62.8 7.7 %collective-permute-done.6 = f32[3,1,8,256]{3,2,1,0:T(8,128)S(1)} collective-permute-done((f32[3,1,8,256]{3,2,1,0:T(8,128)S(1)}, f32[3,1,8,256]{3,2,1,0:T(8,128)S(1)}, u32[]{:S(2)}, u32[]{:S(2)}) %collective-permute-start.6) | collective-permute-done | bytes 24608 | tf_op jit(solution)/shard_map/ppermute | solution.py:23
  75.1 1.3 collective-permute-start.9
  76.4 1.9 collective-permute-start.8
  79.8 5.0 %collective-permute-done.9 = f32[3,32,8,1]{3,2,1,0:T(8,128)S(1)} collective-permute-done((f32[3,32,8,1]{3,2,1,0:T(8,128)S(1)}, f32[3,32,8,1]{3,2,1,0:T(8,128)S(1)}, u32[]{:S(2)}, u32[]{:S(2)}) %collective-permute-start.9) | collective-permute-done | bytes 3104 | tf_op jit(solution)/shard_map/ppermute | solution.py:23
  85.3 1.1 copy-done.2
  86.7 2.0 collective-permute-start.11
  88.8 1.9 collective-permute-start.10
  90.8 4.8 %collective-permute-done.11 = f32[3,32,8,1]{3,2,1,0:T(8,128)S(1)} collective-permute-done((f32[3,32,8,1]{3,2,1,0:T(8,128)S(1)}, f32[3,32,8,1]{3,2,1,0:T(8,128)S(1)}, u32[]{:S(2)}, u32[]{:S(2)}) %collective-permute-start.11) | collective-permute-done | bytes 3104 | tf_op jit(solution)/shard_map/ppermute | solution.py:23
  95.6 7.6 %collective-permute-done.10 = f32[3,1,8,256]{3,2,1,0:T(8,128)S(1)} collective-permute-done((f32[3,1,8,256]{3,2,1,0:T(8,128)S(1)}, f32[3,1,8,256]{3,2,1,0:T(8,128)S(1)}, u32[]{:S(2)}, u32[]{:S(2)}) %collective-permute-start.10) | collective-permute-done | bytes 24608 | tf_op jit(solution)/shard_map/ppermute | solution.py:23
  104.9 1.6 multiply_add_fusion
  107.4 1.3 collective-permute-start.13
  108.7 2.1 collective-permute-start.12
  110.8 1.6 select_reduce_fusion.7
  112.4 5.1 %maximum_add_fusion.2 = f32[4]{0:T(128)S(1)} fusion(f32[1]{0:T(128)} %bitcast.19, f32[1]{0:T(128)} %bitcast.18, f32[1]{0:T(128)} %bitcast.17, f32[1]{0:T(128)} %bitcast.16, f32[1]{0:T(128)} %bitcast.23, f32[1]{0:T(128)} %bitcast.22, f32[1]{0:T(128)} %bitcast.21, f32[1]{0:T(128)} %bitcast.20), kind=kLoop, calls=%fused_computation.132 | loop fusion | flops 28 | bytes 48 | tf_op jit(solution)/shard_map/add | solution.py:185
  118.7 76.3 %psum.16 = f32[4]{0:T(128)S(1)} all-reduce(f32[4]{0:T(128)S(1)} %maximum_add_fusion.2), channel_id=1, replica_groups=mesh['gy'=64,'gz'=4] {'gy','gz'}, use_global_device_ids=true, to_apply=%region_9.10 | all-reduce | flops 4 | bytes 32 | tf_op jit(solution)/shard_map/psum | solution.py:112
  195.4 1.3 maximum_subtract_fusion.11
  198.1 2.1 collective-permute-start.15
  200.2 1.9 collective-permute-start.14
  202.7 6.1 %collective-permute-done.15 = f32[3,32,8,1]{3,2,1,0:T(8,128)S(1)} collective-permute-done((f32[3,32,8,1]{3,2,1,0:T(8,128)S(1)}, f32[3,32,8,1]{3,2,1,0:T(8,128)S(1)}, u32[]{:S(2)}, u32[]{:S(2)}) %collective-permute-start.15) | collective-permute-done | bytes 3104 | tf_op jit(solution)/shard_map/ppermute | solution.py:23
  208.8 5.1 %collective-permute-done.14 = f32[3,1,8,256]{3,2,1,0:T(8,128)S(1)} collective-permute-done((f32[3,1,8,256]{3,2,1,0:T(8,128)S(1)}, f32[3,1,8,256]{3,2,1,0:T(8,128)S(1)}, u32[]{:S(2)}, u32[]{:S(2)}) %collective-permute-start.14) | collective-permute-done | bytes 24608 | tf_op jit(solution)/shard_map/ppermute | solution.py:23
  (130 shorter events, 23.5 us)
Async XLA Ops:
  0.6 2.3 %copy-start = (bf16[3,32,8,256]{3,2,1,0:T(8,128)(2,1)S(1)}, bf16[3,32,8,256]{3,2,1,0:T(8,128)(2,1)}, u32[]{:S(2)}) copy-start(bf16[3,32,8,256]{3,2,1,0:T(8,128)(2,1)} %param.15) | copy-start | bytes 1179652
  1.7 14.2 %collective-permute-start.1 = (f32[3,32,8,1]{3,2,1,0:T(8,128)S(1)}, f32[3,32,8,1]{3,2,1,0:T(8,128)S(1)}, u32[]{:S(2)}, u32[]{:S(2)}) collective-permute-start(f32[3,32,8,1]{3,2,1,0:T(8,128)S(1)} %slice.413), channel_id=1, source_target_pairs={{1,0},{2,1},{3,2},{5,4},{6,5},{7,6},{9,8},{10,9},{11,10},{13,12},{... | collective-permute-start | bytes 9224 | tf_op jit(solution)/shard_map/ppermute | solution.py:23
  3.0 11.0 %copy-start.20 = (f32[4]{0:T(128)S(1)}, f32[4]{0:T(128)}, u32[]{:S(2)}) copy-start(f32[4]{0:T(128)} %param.27) | copy-start | bytes 52
  3.0 12.8 %collective-permute-start = (f32[3,1,8,256]{3,2,1,0:T(8,128)S(1)}, f32[3,1,8,256]{3,2,1,0:T(8,128)S(1)}, u32[]{:S(2)}, u32[]{:S(2)}) collective-permute-start(f32[3,1,8,256]{3,2,1,0:T(8,128)S(1)} %slice.410), channel_id=1, source_target_pairs={{4,0},{8,4},{12,8},{16,12},{20,16},{24,20},{28,24},{32,28},{36,32}... | collective-permute-start | bytes 73736 | tf_op jit(solution)/shard_map/ppermute | solution.py:23
  17.2 9.6 %copy-start.13 = (s32[32,8,256]{2,1,0:T(8,128)S(1)}, s32[32,8,256]{2,1,0:T(8,128)}, u32[]{:S(2)}) copy-start(s32[32,8,256]{2,1,0:T(8,128)} %param.26) | copy-start | bytes 786436
  17.2 9.6 %copy-start.19 = (s32[32,8,256]{2,1,0:T(8,128)S(1)}, s32[32,8,256]{2,1,0:T(8,128)}, u32[]{:S(2)}) copy-start(s32[32,8,256]{2,1,0:T(8,128)} %param.25) | copy-start | bytes 786436
  17.4 13.0 %collective-permute-start.3 = (f32[3,32,8,1]{3,2,1,0:T(8,128)S(1)}, f32[3,32,8,1]{3,2,1,0:T(8,128)S(1)}, u32[]{:S(2)}, u32[]{:S(2)}) collective-permute-start(f32[3,32,8,1]{3,2,1,0:T(8,128)S(1)} %slice.423), channel_id=1, source_target_pairs={{0,1},{1,2},{2,3},{4,5},{5,6},{6,7},{8,9},{9,10},{10,11},{12,13},{... | collective-permute-start | bytes 9224 | tf_op jit(solution)/shard_map/ppermute | solution.py:23
  21.7 17.5 %collective-permute-start.2 = (f32[3,1,8,256]{3,2,1,0:T(8,128)S(1)}, f32[3,1,8,256]{3,2,1,0:T(8,128)S(1)}, u32[]{:S(2)}, u32[]{:S(2)}) collective-permute-start(f32[3,1,8,256]{3,2,1,0:T(8,128)S(1)} %slice.420), channel_id=1, source_target_pairs={{0,4},{4,8},{8,12},{12,16},{16,20},{20,24},{24,28},{28,32},{32,36}... | collective-permute-start | bytes 73736 | tf_op jit(solution)/shard_map/ppermute | solution.py:23
  39.6 1.1 copy-start.4
  42.4 3.4 %copy-start.5 = (f32[2,32,8,256]{3,2,1,0:T(8,128)S(1)}, f32[2,32,8,256]{3,2,1,0:T(8,128)}, u32[]{:S(2)}) copy-start(f32[2,32,8,256]{3,2,1,0:T(8,128)} %param.24) | copy-start | bytes 1572868
  42.5 9.8 %collective-permute-start.5 = (f32[3,32,8,1]{3,2,1,0:T(8,128)S(1)}, f32[3,32,8,1]{3,2,1,0:T(8,128)S(1)}, u32[]{:S(2)}, u32[]{:S(2)}) collective-permute-start(f32[3,32,8,1]{3,2,1,0:T(8,128)S(1)} %slice.437), channel_id=1, source_target_pairs={{1,0},{2,1},{3,2},{5,4},{6,5},{7,6},{9,8},{10,9},{11,10},{13,12},{... | collective-permute-start | bytes 9224 | tf_op jit(solution)/shard_map/ppermute | solution.py:23
  43.9 8.4 %collective-permute-start.4 = (f32[3,1,8,256]{3,2,1,0:T(8,128)S(1)}, f32[3,1,8,256]{3,2,1,0:T(8,128)S(1)}, u32[]{:S(2)}, u32[]{:S(2)}) collective-permute-start(f32[3,1,8,256]{3,2,1,0:T(8,128)S(1)} %slice.434), channel_id=1, source_target_pairs={{4,0},{8,4},{12,8},{16,12},{20,16},{24,20},{28,24},{32,28},{36,32}... | collective-permute-start | bytes 73736 | tf_op jit(solution)/shard_map/ppermute | solution.py:23
  53.0 9.7 %collective-permute-start.7 = (f32[3,32,8,1]{3,2,1,0:T(8,128)S(1)}, f32[3,32,8,1]{3,2,1,0:T(8,128)S(1)}, u32[]{:S(2)}, u32[]{:S(2)}) collective-permute-start(f32[3,32,8,1]{3,2,1,0:T(8,128)S(1)} %slice.447), channel_id=1, source_target_pairs={{0,1},{1,2},{2,3},{4,5},{5,6},{6,7},{8,9},{9,10},{10,11},{12,13},{... | collective-permute-start | bytes 9224 | tf_op jit(solution)/shard_map/ppermute | solution.py:23
  55.0 15.4 %collective-permute-start.6 = (f32[3,1,8,256]{3,2,1,0:T(8,128)S(1)}, f32[3,1,8,256]{3,2,1,0:T(8,128)S(1)}, u32[]{:S(2)}, u32[]{:S(2)}) collective-permute-start(f32[3,1,8,256]{3,2,1,0:T(8,128)S(1)} %slice.444), channel_id=1, source_target_pairs={{0,4},{4,8},{8,12},{12,16},{16,20},{20,24},{24,28},{28,32},{32,36}... | collective-permute-start | bytes 73736 | tf_op jit(solution)/shard_map/ppermute | solution.py:23
  71.6 1.1 copy-start.16
  73.2 1.1 copy-start.6
  73.2 1.4 copy-start.17
  73.3 1.3 copy-start.21
  75.1 9.7 %collective-permute-start.9 = (f32[3,32,8,1]{3,2,1,0:T(8,128)S(1)}, f32[3,32,8,1]{3,2,1,0:T(8,128)S(1)}, u32[]{:S(2)}, u32[]{:S(2)}) collective-permute-start(f32[3,32,8,1]{3,2,1,0:T(8,128)S(1)} %slice.461), channel_id=1, source_target_pairs={{1,0},{2,1},{3,2},{5,4},{6,5},{7,6},{9,8},{10,9},{11,10},{13,12},{... | collective-permute-start | bytes 9224 | tf_op jit(solution)/shard_map/ppermute | solution.py:23
  76.4 8.4 %collective-permute-start.8 = (f32[3,1,8,256]{3,2,1,0:T(8,128)S(1)}, f32[3,1,8,256]{3,2,1,0:T(8,128)S(1)}, u32[]{:S(2)}, u32[]{:S(2)}) collective-permute-start(f32[3,1,8,256]{3,2,1,0:T(8,128)S(1)} %slice.458), channel_id=1, source_target_pairs={{4,0},{8,4},{12,8},{16,12},{20,16},{24,20},{28,24},{32,28},{36,32}... | collective-permute-start | bytes 73736 | tf_op jit(solution)/shard_map/ppermute | solution.py:23
  85.1 1.3 copy-start.2
  85.3 17.9 %copy-start.7 = (f32[1,32,8,256]{3,2,1,0:T(8,128)}, f32[1,32,8,256]{3,2,1,0:T(8,128)S(1)}, u32[]{:S(2)}) copy-start(f32[1,32,8,256]{3,2,1,0:T(8,128)S(1)} %get-tuple-element.59) | copy-start | bytes 786436
  85.3 17.9 %copy-start.9 = (f32[1,32,8,256]{3,2,1,0:T(8,128)}, f32[1,32,8,256]{3,2,1,0:T(8,128)S(1)}, u32[]{:S(2)}) copy-start(f32[1,32,8,256]{3,2,1,0:T(8,128)S(1)} %get-tuple-element.60) | copy-start | bytes 786436
  85.3 17.9 %copy-start.11 = (f32[1,32,8,256]{3,2,1,0:T(8,128)}, f32[1,32,8,256]{3,2,1,0:T(8,128)S(1)}, u32[]{:S(2)}) copy-start(f32[1,32,8,256]{3,2,1,0:T(8,128)S(1)} %get-tuple-element.61) | copy-start | bytes 786436
  86.7 8.9 %collective-permute-start.11 = (f32[3,32,8,1]{3,2,1,0:T(8,128)S(1)}, f32[3,32,8,1]{3,2,1,0:T(8,128)S(1)}, u32[]{:S(2)}, u32[]{:S(2)}) collective-permute-start(f32[3,32,8,1]{3,2,1,0:T(8,128)S(1)} %slice.471), channel_id=1, source_target_pairs={{0,1},{1,2},{2,3},{4,5},{5,6},{6,7},{8,9},{9,10},{10,11},{12,13},{... | collective-permute-start | bytes 9224 | tf_op jit(solution)/shard_map/ppermute | solution.py:23
  88.8 14.5 %collective-permute-start.10 = (f32[3,1,8,256]{3,2,1,0:T(8,128)S(1)}, f32[3,1,8,256]{3,2,1,0:T(8,128)S(1)}, u32[]{:S(2)}, u32[]{:S(2)}) collective-permute-start(f32[3,1,8,256]{3,2,1,0:T(8,128)S(1)} %slice.468), channel_id=1, source_target_pairs={{0,4},{4,8},{8,12},{12,16},{16,20},{20,24},{24,28},{28,32},{32,36}... | collective-permute-start | bytes 73736 | tf_op jit(solution)/shard_map/ppermute | solution.py:23
  107.4 88.0 %collective-permute-start.13 = (f32[3,32,8,1]{3,2,1,0:T(8,128)}, f32[3,32,8,1]{3,2,1,0:T(8,128)}, u32[]{:S(2)}, u32[]{:S(2)}) collective-permute-start(f32[3,32,8,1]{3,2,1,0:T(8,128)} %slice.483), channel_id=1, source_target_pairs={{1,0},{2,1},{3,2},{5,4},{6,5},{7,6},{9,8},{10,9},{11,10},{13,12},{... | collective-permute-start | bytes 9224 | tf_op jit(solution)/shard_map/ppermute | solution.py:23
  108.7 86.7 %collective-permute-start.12 = (f32[3,1,8,256]{3,2,1,0:T(8,128)S(1)}, f32[3,1,8,256]{3,2,1,0:T(8,128)S(1)}, u32[]{:S(2)}, u32[]{:S(2)}) collective-permute-start(f32[3,1,8,256]{3,2,1,0:T(8,128)S(1)} %slice.480), channel_id=1, source_target_pairs={{4,0},{8,4},{12,8},{16,12},{20,16},{24,20},{28,24},{32,28},{36,32}... | collective-permute-start | bytes 73736 | tf_op jit(solution)/shard_map/ppermute | solution.py:23
  196.7 1.1 copy-start.12
  198.0 15.9 %copy-start.1 = (f32[3,32,8,256]{3,2,1,0:T(8,128)}, f32[3,32,8,256]{3,2,1,0:T(8,128)S(1)}, u32[]{:S(2)}) copy-start(f32[3,32,8,256]{3,2,1,0:T(8,128)S(1)} %maximum_add_fusion.1) | copy-start | bytes 2359300
  198.1 10.7 %collective-permute-start.15 = (f32[3,32,8,1]{3,2,1,0:T(8,128)S(1)}, f32[3,32,8,1]{3,2,1,0:T(8,128)S(1)}, u32[]{:S(2)}, u32[]{:S(2)}) collective-permute-start(f32[3,32,8,1]{3,2,1,0:T(8,128)S(1)} %slice.493), channel_id=1, source_target_pairs={{0,1},{1,2},{2,3},{4,5},{5,6},{6,7},{8,9},{9,10},{10,11},{12,13},{... | collective-permute-start | bytes 9224 | tf_op jit(solution)/shard_map/ppermute | solution.py:23
  200.2 13.7 %collective-permute-start.14 = (f32[3,1,8,256]{3,2,1,0:T(8,128)S(1)}, f32[3,1,8,256]{3,2,1,0:T(8,128)S(1)}, u32[]{:S(2)}, u32[]{:S(2)}) collective-permute-start(f32[3,1,8,256]{3,2,1,0:T(8,128)S(1)} %slice.490), channel_id=1, source_target_pairs={{0,4},{4,8},{8,12},{12,16},{16,20},{20,24},{24,28},{28,32},{32,36}... | collective-permute-start | bytes 73736 | tf_op jit(solution)/shard_map/ppermute | solution.py:23
  (7 other events, 6.5 us)
where the time goes:
time: 217 us; the launch traced here: 216 us
  blocking collectives  76.3 us (35%)
  waiting for transfers between devices  56.5 us (26%)
  starting transfers between devices  43.4 us (20%)
  other arithmetic  23.4 us (11%)
  local copies, waits for them, and re-layouts  13.7 us (6%)
  between operations  2.27 us (1%)
    psum x1, blocking collectives, step_total(): return lax.psum(label_sums(material_labels, values, count), ('gy', 'gz'))  76.3 us
    ppermute x16, waiting for transfers between devices, shifted(): return lax.ppermute(block, axis, route)  56.5 us
    ppermute x16, starting transfers between devices, shifted(): return lax.ppermute(block, axis, route)  43.4 us
    unnamed x46, local copies, waits for them, and re-layouts  8.78 us
    add x1, other arithmetic, on_device(): step_total(material_labels, grad_second, count)  5.11 us
  transfers between devices with their start and end apart: 16, of which 9 were waited for; matrix products, arithmetic and copies ran while one was open for 7% of the time, Pallas kernels for 0%

commit v1 on v0

--- a/solution.py
+++ b/solution.py
@@ -109,7 +109,7 @@
 
 
 def step_total(material_labels, values, count):
-    return lax.psum(label_sums(material_labels, values, count), ("gy", "gz"))
+    return jnp.sum(lax.all_gather(label_sums(material_labels, values, count), ("gy", "gz")), axis=0)
 
 
 def on_device(

time: 217 us -> 228 us (1.051)
  local copies, waits for them, and re-layouts: 13.7 us -> 22.2 us
  other arithmetic: 23.4 us -> 27.8 us
    unnamed x0 -> x1, blocking collectives: none -> 76.8 us
    psum x1 -> x0, blocking collectives: 76.3 us -> none  [step_total(): return lax.psum(label_sums(material_labels, values, count), ('gy', 'gz'))]
    unnamed x0 -> x2, other arithmetic: none -> 5.49 us
    add x1 -> x0, other arithmetic: 5.11 us -> none  [on_device(): step_total(material_labels, grad_second, count)]
    unnamed x46 -> x106, local copies, waits for them, and re-layouts: 8.78 us -> 12.4 us
  transfers between devices with their start and end apart: 16 -> 16, of which waited for: 9 -> 9; matrix products, arithmetic and copies ran while one was open for 7% -> 8% of each run, Pallas kernels for 0% -> 0%
where the time goes in v1:
time: 228 us; the launch traced here: 227 us
  blocking collectives  76.8 us (34%)
  waiting for transfers between devices  55.3 us (24%)
  starting transfers between devices  42.7 us (19%)
  other arithmetic  27.8 us (12%)
  local copies, waits for them, and re-layouts  22.2 us (10%)
  between operations  2.53 us (1%)
    unnamed x1, blocking collectives  76.8 us
    ppermute x16, waiting for transfers between devices, shifted(): return lax.ppermute(block, axis, route)  55.3 us
    ppermute x16, starting transfers between devices, shifted(): return lax.ppermute(block, axis, route)  42.7 us
    unnamed x106, local copies, waits for them, and re-layouts  12.4 us
    unnamed x2, other arithmetic  5.49 us
  transfers between devices with their start and end apart: 16, of which 9 were waited for; matrix products, arithmetic and copies ran while one was open for 8% of the time, Pallas kernels for 0%

profile of v1, /device:TPU:2, one launch (start us, length us, event | category | flops | bytes accessed | tf_op | source)
XLA Modules:
  0.0 227.3 jit_solution(12572453001096764230)
XLA Ops:
  1.7 1.3 collective-permute-start.1
  3.0 11.0 %collective-permute-start = (f32[3,1,8,256]{3,2,1,0:T(8,128)S(1)}, f32[3,1,8,256]{3,2,1,0:T(8,128)S(1)}, u32[]{:S(2)}, u32[]{:S(2)}) collective-permute-start(f32[3,1,8,256]{3,2,1,0:T(8,128)S(1)} %slice.410), channel_id=1, source_target_pairs={{4,0},{8,4},{12,8},{16,12},{20,16},{24,20},{28,24},{32,28},{36,32}... | collective-permute-start | bytes 73736 | tf_op jit(solution)/shard_map/ppermute | solution.py:23
  17.5 4.3 %collective-permute-start.3 = (f32[3,32,8,1]{3,2,1,0:T(8,128)S(1)}, f32[3,32,8,1]{3,2,1,0:T(8,128)S(1)}, u32[]{:S(2)}, u32[]{:S(2)}) collective-permute-start(f32[3,32,8,1]{3,2,1,0:T(8,128)S(1)} %slice.423), channel_id=1, source_target_pairs={{0,1},{1,2},{2,3},{4,5},{5,6},{6,7},{8,9},{9,10},{10,11},{12,13},{... | collective-permute-start | bytes 9224 | tf_op jit(solution)/shard_map/ppermute | solution.py:23
  21.8 5.1 %collective-permute-start.2 = (f32[3,1,8,256]{3,2,1,0:T(8,128)S(1)}, f32[3,1,8,256]{3,2,1,0:T(8,128)S(1)}, u32[]{:S(2)}, u32[]{:S(2)}) collective-permute-start(f32[3,1,8,256]{3,2,1,0:T(8,128)S(1)} %slice.420), channel_id=1, source_target_pairs={{0,4},{4,8},{8,12},{12,16},{16,20},{20,24},{24,28},{28,32},{32,36}... | collective-permute-start | bytes 73736 | tf_op jit(solution)/shard_map/ppermute | solution.py:23
  26.9 3.5 %select_add_fusion.2 = (f32[32,8,256]{2,1,0:T(8,128)S(1)}, pred[32,8,256]{2,1,0:T(8,128)(4,1)}, pred[32,8,256]{2,1,0:T(8,128)(4,1)}, pred[32,8,256]{2,1,0:T(8,12...) fusion(f32[]{:T(128)} %bitcast.6, f32[]{:T(128)} %bitcast.5, f32[]{:T(128)} %bitcast.4, f32[]{:T(128)} %bitcast.3, ...), kind=kLoop, calls=%fused_computation.118 | loop fusion | flops 983040 | bytes 1835024 | tf_op jit(solution)/shard_map/add | solution.py:96
  31.2 8.1 %collective-permute-done.2 = f32[3,1,8,256]{3,2,1,0:T(8,128)S(1)} collective-permute-done((f32[3,1,8,256]{3,2,1,0:T(8,128)S(1)}, f32[3,1,8,256]{3,2,1,0:T(8,128)S(1)}, u32[]{:S(2)}, u32[]{:S(2)}) %collective-permute-start.2) | collective-permute-done | bytes 24608 | tf_op jit(solution)/shard_map/ppermute | solution.py:23
  45.9 1.9 collective-permute-start.4
  49.2 5.3 %collective-permute-done.5 = f32[3,32,8,1]{3,2,1,0:T(8,128)} collective-permute-done((f32[3,32,8,1]{3,2,1,0:T(8,128)}, f32[3,32,8,1]{3,2,1,0:T(8,128)}, u32[]{:S(2)}, u32[]{:S(2)}) %collective-permute-start.5) | collective-permute-done | bytes 3104 | tf_op jit(solution)/shard_map/ppermute | solution.py:23
  54.6 1.3 maximum_subtract_fusion.3
  57.4 2.0 collective-permute-start.7
  59.5 1.9 collective-permute-start.6
  61.7 5.6 %collective-permute-done.7 = f32[3,32,8,1]{3,2,1,0:T(8,128)S(1)} collective-permute-done((f32[3,32,8,1]{3,2,1,0:T(8,128)S(1)}, f32[3,32,8,1]{3,2,1,0:T(8,128)S(1)}, u32[]{:S(2)}, u32[]{:S(2)}) %collective-permute-start.7) | collective-permute-done | bytes 3104 | tf_op jit(solution)/shard_map/ppermute | solution.py:23
  67.3 7.4 %collective-permute-done.6 = f32[3,1,8,256]{3,2,1,0:T(8,128)S(1)} collective-permute-done((f32[3,1,8,256]{3,2,1,0:T(8,128)S(1)}, f32[3,1,8,256]{3,2,1,0:T(8,128)S(1)}, u32[]{:S(2)}, u32[]{:S(2)}) %collective-permute-start.6) | collective-permute-done | bytes 24608 | tf_op jit(solution)/shard_map/ppermute | solution.py:23
  79.6 1.3 collective-permute-start.9
  80.9 1.9 collective-permute-start.8
  84.6 4.7 %collective-permute-done.9 = f32[3,32,8,1]{3,2,1,0:T(8,128)S(1)} collective-permute-done((f32[3,32,8,1]{3,2,1,0:T(8,128)S(1)}, f32[3,32,8,1]{3,2,1,0:T(8,128)S(1)}, u32[]{:S(2)}, u32[]{:S(2)}) %collective-permute-start.9) | collective-permute-done | bytes 3104 | tf_op jit(solution)/shard_map/ppermute | solution.py:23
  91.2 1.8 collective-permute-start.11
  93.0 1.9 collective-permute-start.10
  95.1 5.3 %collective-permute-done.11 = f32[3,32,8,1]{3,2,1,0:T(8,128)S(1)} collective-permute-done((f32[3,32,8,1]{3,2,1,0:T(8,128)S(1)}, f32[3,32,8,1]{3,2,1,0:T(8,128)S(1)}, u32[]{:S(2)}, u32[]{:S(2)}) %collective-permute-start.11) | collective-permute-done | bytes 3104 | tf_op jit(solution)/shard_map/ppermute | solution.py:23
  100.4 7.1 %collective-permute-done.10 = f32[3,1,8,256]{3,2,1,0:T(8,128)S(1)} collective-permute-done((f32[3,1,8,256]{3,2,1,0:T(8,128)S(1)}, f32[3,1,8,256]{3,2,1,0:T(8,128)S(1)}, u32[]{:S(2)}, u32[]{:S(2)}) %collective-permute-start.10) | collective-permute-done | bytes 24608 | tf_op jit(solution)/shard_map/ppermute | solution.py:23
  110.5 1.6 multiply_add_fusion
  113.5 1.4 collective-permute-start.13
  115.0 1.9 collective-permute-start.12
  117.0 1.6 select_reduce_fusion.7
  118.5 2.8 %maximum_dynamic-update-slice_fusion.1 = f32[1024]{0:T(1024)S(1)} fusion(f32[1024]{0:T(1024)S(1)} %broadcast.161.clone.1, u32[]{:T(128)S(6)} %multiply.9, f32[1]{0:T(128)} %bitcast.23, f32[1]{0:T(128)} %bitcast.22, f32[1]{0:T(128)} %bitcast.21, f32[1]{0:T(128)} %bitcast.20), kind=kLoop, calls=%fused_computation.133 | loop fusion | flops 12 | bytes 532
  122.5 2.7 %maximum_dynamic-update-slice_fusion = f32[1024]{0:T(1024)S(1)} fusion(f32[1024]{0:T(1024)S(1)} %broadcast.161.clone, u32[]{:T(128)S(6)} %multiply.9, f32[1]{0:T(128)} %bitcast.19, f32[1]{0:T(128)} %bitcast.18, f32[1]{0:T(128)} %bitcast.17, f32[1]{0:T(128)} %bitcast.16), kind=kLoop, calls=%fused_computation.132 | loop fusion | flops 12 | bytes 532
  128.3 76.8 %all-reduce.28 = (f32[1024]{0:T(1024)S(1)}, f32[1024]{0:T(1024)S(1)}) all-reduce(f32[1024]{0:T(1024)S(1)} %maximum_dynamic-update-slice_fusion, f32[1024]{0:T(1024)S(1)} %maximum_dynamic-update-slice_fusion.1), channel_id=2, replica_groups=mesh['gy'=64,'gz'=4] {'gy','gz'}, use_global_device_ids=true, to_apply=%add.26 | all-reduce | flops 2048 | bytes 16384
  205.4 2.0 maximum_subtract_fusion.11
  208.8 1.6 collective-permute-start.15
  210.4 1.9 collective-permute-start.14
  212.9 6.1 %collective-permute-done.15 = f32[3,32,8,1]{3,2,1,0:T(8,128)S(1)} collective-permute-done((f32[3,32,8,1]{3,2,1,0:T(8,128)S(1)}, f32[3,32,8,1]{3,2,1,0:T(8,128)S(1)}, u32[]{:S(2)}, u32[]{:S(2)}) %collective-permute-start.15) | collective-permute-done | bytes 3104 | tf_op jit(solution)/shard_map/ppermute | solution.py:23
  219.0 5.6 %collective-permute-done.14 = f32[3,1,8,256]{3,2,1,0:T(8,128)S(1)} collective-permute-done((f32[3,1,8,256]{3,2,1,0:T(8,128)S(1)}, f32[3,1,8,256]{3,2,1,0:T(8,128)S(1)}, u32[]{:S(2)}, u32[]{:S(2)}) %collective-permute-start.14) | collective-permute-done | bytes 24608 | tf_op jit(solution)/shard_map/ppermute | solution.py:23
  (195 shorter events, 35.9 us)
Async XLA Ops:
  1.7 14.2 %collective-permute-start.1 = (f32[3,32,8,1]{3,2,1,0:T(8,128)S(1)}, f32[3,32,8,1]{3,2,1,0:T(8,128)S(1)}, u32[]{:S(2)}, u32[]{:S(2)}) collective-permute-start(f32[3,32,8,1]{3,2,1,0:T(8,128)S(1)} %slice.413), channel_id=1, source_target_pairs={{1,0},{2,1},{3,2},{5,4},{6,5},{7,6},{9,8},{10,9},{11,10},{13,12},{... | collective-permute-start | bytes 9224 | tf_op jit(solution)/shard_map/ppermute | solution.py:23
  3.0 11.0 %copy-start.49 = (f32[4]{0:T(128)S(1)}, f32[4]{0:T(128)}, u32[]{:S(2)}) copy-start(f32[4]{0:T(128)} %param.27) | copy-start | bytes 52
  3.0 12.9 %collective-permute-start = (f32[3,1,8,256]{3,2,1,0:T(8,128)S(1)}, f32[3,1,8,256]{3,2,1,0:T(8,128)S(1)}, u32[]{:S(2)}, u32[]{:S(2)}) collective-permute-start(f32[3,1,8,256]{3,2,1,0:T(8,128)S(1)} %slice.410), channel_id=1, source_target_pairs={{4,0},{8,4},{12,8},{16,12},{20,16},{24,20},{28,24},{32,28},{36,32}... | collective-permute-start | bytes 73736 | tf_op jit(solution)/shard_map/ppermute | solution.py:23
  15.8 11.0 %copy-start.26 = (f32[2,32,8,256]{3,2,1,0:T(8,128)}, f32[2,32,8,256]{3,2,1,0:T(8,128)S(1)}, u32[]{:S(2)}) copy-start(f32[2,32,8,256]{3,2,1,0:T(8,128)S(1)} %convert_element_type.25) | copy-start | bytes 1572868
  16.3 23.0 %copy-start.12 = (f32[1,32,8,256]{3,2,1,0:T(8,128)}, f32[1,32,8,256]{3,2,1,0:T(8,128)S(1)}, u32[]{:S(2)}) copy-start(f32[1,32,8,256]{3,2,1,0:T(8,128)S(1)} %get-tuple-element.83) | copy-start | bytes 786436
  16.3 23.0 %copy-start.14 = (f32[1,32,8,256]{3,2,1,0:T(8,128)}, f32[1,32,8,256]{3,2,1,0:T(8,128)S(1)}, u32[]{:S(2)}) copy-start(f32[1,32,8,256]{3,2,1,0:T(8,128)S(1)} %get-tuple-element.84) | copy-start | bytes 786436
  17.3 9.6 %copy-start.20 = (s32[32,8,256]{2,1,0:T(8,128)S(1)}, s32[32,8,256]{2,1,0:T(8,128)}, u32[]{:S(2)}) copy-start(s32[32,8,256]{2,1,0:T(8,128)} %param.26) | copy-start | bytes 786436
  17.3 9.6 %copy-start.48 = (s32[32,8,256]{2,1,0:T(8,128)S(1)}, s32[32,8,256]{2,1,0:T(8,128)}, u32[]{:S(2)}) copy-start(s32[32,8,256]{2,1,0:T(8,128)} %param.25) | copy-start | bytes 786436
  17.5 13.7 %collective-permute-start.3 = (f32[3,32,8,1]{3,2,1,0:T(8,128)S(1)}, f32[3,32,8,1]{3,2,1,0:T(8,128)S(1)}, u32[]{:S(2)}, u32[]{:S(2)}) collective-permute-start(f32[3,32,8,1]{3,2,1,0:T(8,128)S(1)} %slice.423), channel_id=1, source_target_pairs={{0,1},{1,2},{2,3},{4,5},{5,6},{6,7},{8,9},{9,10},{10,11},{12,13},{... | collective-permute-start | bytes 9224 | tf_op jit(solution)/shard_map/ppermute | solution.py:23
  21.8 17.5 %collective-permute-start.2 = (f32[3,1,8,256]{3,2,1,0:T(8,128)S(1)}, f32[3,1,8,256]{3,2,1,0:T(8,128)S(1)}, u32[]{:S(2)}, u32[]{:S(2)}) collective-permute-start(f32[3,1,8,256]{3,2,1,0:T(8,128)S(1)} %slice.420), channel_id=1, source_target_pairs={{0,4},{4,8},{8,12},{12,16},{16,20},{20,24},{24,28},{28,32},{32,36}... | collective-permute-start | bytes 73736 | tf_op jit(solution)/shard_map/ppermute | solution.py:23
  43.2 4.6 %copy-start.7 = (f32[2,32,8,256]{3,2,1,0:T(8,128)S(1)}, f32[2,32,8,256]{3,2,1,0:T(8,128)}, u32[]{:S(2)}) copy-start(f32[2,32,8,256]{3,2,1,0:T(8,128)} %param.24) | copy-start | bytes 1572868
  44.6 10.0 %collective-permute-start.5 = (f32[3,32,8,1]{3,2,1,0:T(8,128)}, f32[3,32,8,1]{3,2,1,0:T(8,128)}, u32[]{:S(2)}, u32[]{:S(2)}) collective-permute-start(f32[3,32,8,1]{3,2,1,0:T(8,128)} %slice.437), channel_id=1, source_target_pairs={{1,0},{2,1},{3,2},{5,4},{6,5},{7,6},{9,8},{10,9},{11,10},{13,12},{... | collective-permute-start | bytes 9224 | tf_op jit(solution)/shard_map/ppermute | solution.py:23
  45.9 8.7 %collective-permute-start.4 = (f32[3,1,8,256]{3,2,1,0:T(8,128)}, f32[3,1,8,256]{3,2,1,0:T(8,128)}, u32[]{:S(2)}, u32[]{:S(2)}) collective-permute-start(f32[3,1,8,256]{3,2,1,0:T(8,128)} %slice.434), channel_id=1, source_target_pairs={{4,0},{8,4},{12,8},{16,12},{20,16},{24,20},{28,24},{32,28},{36,32}... | collective-permute-start | bytes 73736 | tf_op jit(solution)/shard_map/ppermute | solution.py:23
  48.7 34.1 %copy-start.28 = (f32[1,32,8,256]{3,2,1,0:T(8,128)}, f32[1,32,8,256]{3,2,1,0:T(8,128)S(1)}, u32[]{:S(2)}) copy-start(f32[1,32,8,256]{3,2,1,0:T(8,128)S(1)} %get-tuple-element.93) | copy-start | bytes 786436
  48.7 34.2 %copy-start.30 = (f32[1,32,8,256]{3,2,1,0:T(8,128)}, f32[1,32,8,256]{3,2,1,0:T(8,128)S(1)}, u32[]{:S(2)}) copy-start(f32[1,32,8,256]{3,2,1,0:T(8,128)S(1)} %get-tuple-element.94) | copy-start | bytes 786436
  48.7 34.2 %copy-start.32 = (f32[1,32,8,256]{3,2,1,0:T(8,128)}, f32[1,32,8,256]{3,2,1,0:T(8,128)S(1)}, u32[]{:S(2)}) copy-start(f32[1,32,8,256]{3,2,1,0:T(8,128)S(1)} %get-tuple-element.95) | copy-start | bytes 786436
  57.0 4.4 %copy-start.40 = (f32[32,8,256]{2,1,0:T(8,128)S(1)}, f32[32,8,256]{2,1,0:T(8,128)}, u32[]{:S(2)}) copy-start(f32[32,8,256]{2,1,0:T(8,128)} %get-tuple-element.29) | copy-start | bytes 786436
  57.4 9.9 %collective-permute-start.7 = (f32[3,32,8,1]{3,2,1,0:T(8,128)S(1)}, f32[3,32,8,1]{3,2,1,0:T(8,128)S(1)}, u32[]{:S(2)}, u32[]{:S(2)}) collective-permute-start(f32[3,32,8,1]{3,2,1,0:T(8,128)S(1)} %slice.447), channel_id=1, source_target_pairs={{0,1},{1,2},{2,3},{4,5},{5,6},{6,7},{8,9},{9,10},{10,11},{12,13},{... | collective-permute-start | bytes 9224 | tf_op jit(solution)/shard_map/ppermute | solution.py:23
  59.5 15.3 %collective-permute-start.6 = (f32[3,1,8,256]{3,2,1,0:T(8,128)S(1)}, f32[3,1,8,256]{3,2,1,0:T(8,128)S(1)}, u32[]{:S(2)}, u32[]{:S(2)}) collective-permute-start(f32[3,1,8,256]{3,2,1,0:T(8,128)S(1)} %slice.444), channel_id=1, source_target_pairs={{0,4},{4,8},{8,12},{12,16},{16,20},{20,24},{24,28},{28,32},{32,36}... | collective-permute-start | bytes 73736 | tf_op jit(solution)/shard_map/ppermute | solution.py:23
  79.6 9.7 %collective-permute-start.9 = (f32[3,32,8,1]{3,2,1,0:T(8,128)S(1)}, f32[3,32,8,1]{3,2,1,0:T(8,128)S(1)}, u32[]{:S(2)}, u32[]{:S(2)}) collective-permute-start(f32[3,32,8,1]{3,2,1,0:T(8,128)S(1)} %slice.461), channel_id=1, source_target_pairs={{1,0},{2,1},{3,2},{5,4},{6,5},{7,6},{9,8},{10,9},{11,10},{13,12},{... | collective-permute-start | bytes 9224 | tf_op jit(solution)/shard_map/ppermute | solution.py:23
  80.9 8.4 %collective-permute-start.8 = (f32[3,1,8,256]{3,2,1,0:T(8,128)S(1)}, f32[3,1,8,256]{3,2,1,0:T(8,128)S(1)}, u32[]{:S(2)}, u32[]{:S(2)}) collective-permute-start(f32[3,1,8,256]{3,2,1,0:T(8,128)S(1)} %slice.458), channel_id=1, source_target_pairs={{4,0},{8,4},{12,8},{16,12},{20,16},{24,20},{28,24},{32,28},{36,32}... | collective-permute-start | bytes 73736 | tf_op jit(solution)/shard_map/ppermute | solution.py:23
  89.7 17.8 %copy-start.16 = (f32[1,32,8,256]{3,2,1,0:T(8,128)}, f32[1,32,8,256]{3,2,1,0:T(8,128)S(1)}, u32[]{:S(2)}) copy-start(f32[1,32,8,256]{3,2,1,0:T(8,128)S(1)} %get-tuple-element.62) | copy-start | bytes 786436
  89.7 17.8 %copy-start.18 = (f32[1,32,8,256]{3,2,1,0:T(8,128)}, f32[1,32,8,256]{3,2,1,0:T(8,128)S(1)}, u32[]{:S(2)}) copy-start(f32[1,32,8,256]{3,2,1,0:T(8,128)S(1)} %get-tuple-element.63) | copy-start | bytes 786436
  91.2 9.2 %collective-permute-start.11 = (f32[3,32,8,1]{3,2,1,0:T(8,128)S(1)}, f32[3,32,8,1]{3,2,1,0:T(8,128)S(1)}, u32[]{:S(2)}, u32[]{:S(2)}) collective-permute-start(f32[3,32,8,1]{3,2,1,0:T(8,128)S(1)} %slice.471), channel_id=1, source_target_pairs={{0,1},{1,2},{2,3},{4,5},{5,6},{6,7},{8,9},{9,10},{10,11},{12,13},{... | collective-permute-start | bytes 9224 | tf_op jit(solution)/shard_map/ppermute | solution.py:23
  93.0 14.4 %collective-permute-start.10 = (f32[3,1,8,256]{3,2,1,0:T(8,128)S(1)}, f32[3,1,8,256]{3,2,1,0:T(8,128)S(1)}, u32[]{:S(2)}, u32[]{:S(2)}) collective-permute-start(f32[3,1,8,256]{3,2,1,0:T(8,128)S(1)} %slice.468), channel_id=1, source_target_pairs={{0,4},{4,8},{8,12},{12,16},{16,20},{20,24},{24,28},{28,32},{32,36}... | collective-permute-start | bytes 73736 | tf_op jit(solution)/shard_map/ppermute | solution.py:23
  113.5 91.9 %collective-permute-start.13 = (f32[3,32,8,1]{3,2,1,0:T(8,128)}, f32[3,32,8,1]{3,2,1,0:T(8,128)}, u32[]{:S(2)}, u32[]{:S(2)}) collective-permute-start(f32[3,32,8,1]{3,2,1,0:T(8,128)} %slice.483), channel_id=1, source_target_pairs={{1,0},{2,1},{3,2},{5,4},{6,5},{7,6},{9,8},{10,9},{11,10},{13,12},{... | collective-permute-start | bytes 9224 | tf_op jit(solution)/shard_map/ppermute | solution.py:23
  115.0 90.5 %collective-permute-start.12 = (f32[3,1,8,256]{3,2,1,0:T(8,128)}, f32[3,1,8,256]{3,2,1,0:T(8,128)}, u32[]{:S(2)}, u32[]{:S(2)}) collective-permute-start(f32[3,1,8,256]{3,2,1,0:T(8,128)} %slice.480), channel_id=1, source_target_pairs={{4,0},{8,4},{12,8},{16,12},{20,16},{24,20},{28,24},{32,28},{36,32}... | collective-permute-start | bytes 73736 | tf_op jit(solution)/shard_map/ppermute | solution.py:23
  116.9 4.4 %copy-start.29 = (f32[1,32,8,256]{3,2,1,0:T(8,128)S(1)}, f32[1,32,8,256]{3,2,1,0:T(8,128)}, u32[]{:S(2)}) copy-start(f32[1,32,8,256]{3,2,1,0:T(8,128)} %copy-done.28) | copy-start | bytes 786436
  116.9 4.4 %copy-start.31 = (f32[1,32,8,256]{3,2,1,0:T(8,128)S(1)}, f32[1,32,8,256]{3,2,1,0:T(8,128)}, u32[]{:S(2)}) copy-start(f32[1,32,8,256]{3,2,1,0:T(8,128)} %copy-done.30) | copy-start | bytes 786436
  208.6 16.0 %copy-start.1 = (f32[3,32,8,256]{3,2,1,0:T(8,128)}, f32[3,32,8,256]{3,2,1,0:T(8,128)S(1)}, u32[]{:S(2)}) copy-start(f32[3,32,8,256]{3,2,1,0:T(8,128)S(1)} %maximum_add_fusion.1) | copy-start | bytes 2359300
  208.8 10.2 %collective-permute-start.15 = (f32[3,32,8,1]{3,2,1,0:T(8,128)S(1)}, f32[3,32,8,1]{3,2,1,0:T(8,128)S(1)}, u32[]{:S(2)}, u32[]{:S(2)}) collective-permute-start(f32[3,32,8,1]{3,2,1,0:T(8,128)S(1)} %slice.493), channel_id=1, source_target_pairs={{0,1},{1,2},{2,3},{4,5},{5,6},{6,7},{8,9},{9,10},{10,11},{12,13},{... | collective-permute-start | bytes 9224 | tf_op jit(solution)/shard_map/ppermute | solution.py:23
  210.4 14.2 %collective-permute-start.14 = (f32[3,1,8,256]{3,2,1,0:T(8,128)S(1)}, f32[3,1,8,256]{3,2,1,0:T(8,128)S(1)}, u32[]{:S(2)}, u32[]{:S(2)}) collective-permute-start(f32[3,1,8,256]{3,2,1,0:T(8,128)S(1)} %slice.490), channel_id=1, source_target_pairs={{0,4},{4,8},{8,12},{12,16},{16,20},{20,24},{24,28},{28,32},{32,36}... | collective-permute-start | bytes 73736 | tf_op jit(solution)/shard_map/ppermute | solution.py:23
  (36 other events, 63.1 us)
